TPU v7x, 128 devices: a whole 4x4x4 slice. The times are simulated.
128 devices in a mesh: dp: 16 (over x, y), expert: 8 (over z, core).
Axes of the slice: x: 4, y: 4, z: 4, core: 2. Of those that a mesh axis runs over, the one named last changes fastest.
Arguments:
- context: bfloat16 [8192, 4096], P('dp'), may hold values from -6 to 6
- out_weight: bfloat16 [4096, 4096], P('dp', 'expert'), may hold values from -0.09375 to 0.09375
- residual: bfloat16 [8192, 4096], P('dp', 'expert'), may hold values from -6 to 6
- gate_weight: bfloat16 [8, 4096, 8192], P('expert', None, 'dp'), may hold values from -0.09375 to 0.09375
- up_weight: bfloat16 [8, 4096, 8192], P('expert', None, 'dp'), may hold values from -0.09375 to 0.09375
- down_weight: bfloat16 [8, 8192, 4096], P('expert', 'dp'), may hold values from -0.0625 to 0.0625
- gate_values: float32 [8, 512], P('expert'), may hold values from 0.2 to 1
- chosen_blocks: int32 [8, 4], replicated, may hold values from 0 to 63, as said below
- block_counts: int32 [8], replicated, may hold values from 1 to 4, as said below
Outputs:
- mixed: bfloat16 [8192, 4096], P('dp', 'expert')
Inputs may be any that keep to these rules, and one draw needn't show every extreme that they name: `chosen_blocks`: within one expert the 4 block numbers are distinct; slots from block_counts on are unused but hold valid block numbers. `block_counts`: some expert uses all 4 slots.
All inputs are finite; a program needn't handle non-finite values.
Results may differ from a plain program's by a relative error of at most 0.008.
Values may be sent and summed in bfloat16 or wider, within the bound.
A program may use at most 128 MiB of HBM per device.

v0:
```python
import jax
import jax.numpy as jnp
from jax import lax
from jax.sharding import PartitionSpec as P

BLK = 128
CAP = 4


def body(
    context,
    out_weight,
    residual,
    gate_weight,
    up_weight,
    down_weight,
    gate_values,
    chosen_blocks,
    block_counts,
):
    n_dp = lax.axis_size("dp")
    n_expert = lax.axis_size("expert")
    local_tokens = context.shape[0]
    local_width = residual.shape[1]
    model_width = context.shape[1]
    local_blocks = local_tokens // BLK
    n_blocks = local_blocks * n_dp
    piece = BLK // n_dp
    my_expert = lax.axis_index("expert")
    projected = jnp.dot(
        context,
        lax.all_gather(out_weight, "dp", axis=0, tiled=True),
        preferred_element_type=jnp.float32,
    )
    attended = (residual.astype(jnp.float32) + projected).astype(jnp.bfloat16)
    split = attended.reshape(local_blocks, n_dp, piece, local_width).transpose(1, 0, 2, 3)
    pieces = lax.all_to_all(split, "dp", 0, 0, tiled=True)
    pieces = pieces.reshape(n_blocks, piece, local_width)
    slots = jnp.take(pieces, chosen_blocks.reshape(-1), axis=0)
    slots = slots.reshape(n_expert, CAP, piece, local_width)
    mine = lax.all_to_all(slots, "expert", 0, 3, tiled=True)
    mine = mine.reshape(CAP * piece, model_width)
    picked = lax.all_gather(mine, "dp", axis=0, tiled=True)
    w_gate = gate_weight[0]
    w_up = up_weight[0]
    w_down = down_weight[0]
    gate_row = gate_values[0]
    my_count = lax.dynamic_index_in_dim(block_counts, my_expert, 0, keepdims=False)
    live = jnp.arange(CAP * BLK) // BLK < my_count
    scale = jnp.where(live, gate_row, jnp.zeros_like(gate_row))
    scale = scale.reshape(CAP, n_dp, piece).transpose(1, 0, 2).reshape(-1)
    gate = jnp.dot(picked, w_gate, preferred_element_type=jnp.float32)
    upper = jnp.dot(picked, w_up, preferred_element_type=jnp.float32)
    hidden = (jax.nn.silu(gate) * upper).astype(jnp.bfloat16)
    part = jnp.dot(hidden, w_down, preferred_element_type=jnp.float32)
    part = (part * scale[:, None]).astype(jnp.bfloat16)
    summed = lax.psum_scatter(
        part.reshape(n_dp, CAP * piece, model_width), "dp", scatter_dimension=0, tiled=True
    )
    summed = summed.reshape(CAP * piece, n_expert, local_width).transpose(1, 0, 2)
    outs = lax.all_to_all(summed, "expert", 0, 0, tiled=True)
    outs = outs.reshape(n_expert * CAP, piece * local_width)
    selector = chosen_blocks.reshape(-1)[None, :] == jnp.arange(n_blocks)[:, None]
    added = jnp.dot(selector.astype(jnp.bfloat16), outs, preferred_element_type=jnp.float32)
    added = added.reshape(n_dp, local_blocks, piece, local_width)
    back = lax.all_to_all(added, "dp", 0, 0, tiled=True)
    back = back.transpose(1, 0, 2, 3).reshape(local_tokens, local_width)
    total = attended.astype(jnp.float32) + back
    return total.astype(jnp.bfloat16)


def solution(mesh):
    in_specs = (
        P("dp", None),
        P("dp", "expert"),
        P("dp", "expert"),
        P("expert", None, "dp"),
        P("expert", None, "dp"),
        P("expert", "dp", None),
        P("expert", None),
        P(),
        P(),
    )
    out_specs = P("dp", "expert")
    return jax.shard_map(body, mesh=mesh, in_specs=in_specs, out_specs=out_specs, check_vma=False)
```

profile of v0, /device:TPU:0, one launch (start us, length us, event | category | flops | bytes accessed | tf_op | source)
XLA Modules:
  0.0 281.9 jit_solution(4458407969886781237)
XLA Ops:
  6.5 0.7 all-gather.3.cloned.1.call-update
  7.3 0.8 copy.29
  8.1 55.3 %all-gather.3.cloned.1.call-done = bf16[4096,512]{1,0:T(8,128)(2,1)} async-done(((bf16[256,512]{1,0:T(8,128)(2,1)}), bf16[4096,512]{1,0:T(8,128)(2,1)}) %all-gather.3.cloned.1.call-update) | async-done | bytes 4194320 | tf_op jit(solution)/shard_map/all_gather | solution.py:32
  63.4 5.8 %fusion.8 = bf16[512,512]{1,0:T(8,128)(2,1)S(1)} fusion(bf16[512,4096]{1,0:T(8,128)(2,1)} %param.9, bf16[4096,512]{1,0:T(8,128)(2,1)} %all-gather.3.cloned.1.call-done, bf16[512,512]{1,0:T(8,128)(2,1)} %param.11), kind=kOutput, calls=%fused_computation.9 | convolution fusion | flops 2148270080 | bytes 9437184 | tf_op jit(solution)/shard_map/dot_general | solution.py:30
  69.3 0.8 copy.49
  70.1 5.3 %all-to-all-start = ((bf16[16,4,8,512]{3,2,1,0:T(8,128)(2,1)}), bf16[16,4,8,512]{3,2,1,0:T(8,128)(2,1)S(1)}, u32[]{:S(2)}, u32[]{:S(2)}) async-start(bf16[16,4,8,512]{3,2,1,0:T(8,128)(2,1)} %bitcast.60), calls=%async_computation | async-start | bytes 1048576 | tf_op jit(solution)/shard_map/all_to_all | solution.py:37
  75.5 0.1 copy.30
  75.6 11.3 %all-to-all-done = bf16[16,4,8,512]{3,2,1,0:T(8,128)(2,1)S(1)} async-done(((bf16[16,4,8,512]{3,2,1,0:T(8,128)(2,1)}), bf16[16,4,8,512]{3,2,1,0:T(8,128)(2,1)S(1)}, u32[]{:S(2)}, u32[]{:S(2)}) %all-to-all-start) | async-done | bytes 524320 | tf_op jit(solution)/shard_map/all_to_all | solution.py:37
  86.9 0.6 gather_fusion
  87.4 0.1 broadcast_select_fusion
  87.6 11.8 %all_to_all.30 = bf16[8,4,8,512]{3,2,1,0:T(8,128)(2,1)S(1)} all-to-all(bf16[8,4,8,512]{3,2,1,0:T(8,128)(2,1)S(1)} %broadcast_select_fusion), channel_id=1, replica_groups=mesh['dp'=16,'expert'=8] {'expert'}, dimensions={0} | all-to-all | bytes 524288 | tf_op jit(solution)/shard_map/all_to_all | solution.py:41
  99.3 0.1 copy.50
  99.5 0.8 copy.41
  100.3 0.6 broadcast.96
  100.9 0.7 reduce.3
  101.7 0.7 dynamic_slice.4
  102.4 0.7 select_bitcast_fusion
  103.1 0.1 mul.19
  103.2 44.6 %all-gather.5.cloned.1.call-done = bf16[512,4096]{1,0:T(8,128)(2,1)} async-done(((bf16[32,4096]{1,0:T(8,128)(2,1)}), bf16[512,4096]{1,0:T(8,128)(2,1)}) %all-gather.5.cloned.1.call-update) | async-done | bytes 4194320 | tf_op jit(solution)/shard_map/all_gather | solution.py:43
  147.8 5.9 %fusion.3 = f32[512,512]{1,0:T(8,128)S(1)} fusion(bf16[512,4096]{1,0:T(8,128)(2,1)} %all-gather.5.cloned.1.call-done, bf16[1,4096,512]{2,1,0:T(8,128)(2,1)} %param.12), kind=kOutput, calls=%fused_computation.5 | convolution fusion | flops 2147483648 | bytes 9437184 | tf_op jit(solution)/shard_map/dot_general | solution.py:52
  153.8 2.4 fusion.9
  156.2 4.3 %multiply_convert_fusion = bf16[512,4096]{1,0:T(8,128)(2,1)} fusion(bf16[512,512]{1,0:T(8,128)(2,1)S(1)} %fusion.9, bf16[1,512,4096]{2,1,0:T(8,128)(2,1)S(1)} %copy-done.3, f32[512]{0:T(512)S(1)} %mul.19), kind=kOutput, calls=%fused_computation.1 | convolution fusion | flops 2151677952 | bytes 8914944 | tf_op jit(solution)/shard_map/dot_general | solution.py:55
  160.6 77.4 %reduce-scatter.4.cloned.1.call-done = bf16[1,32,4096]{2,1,0:T(8,128)(2,1)} async-done(((bf16[16,32,4096]{2,1,0:T(8,128)(2,1)}), bf16[1,32,4096]{2,1,0:T(8,128)(2,1)}) %reduce-scatter.4.cloned.1.call-update) | async-done | bytes 262160
  237.9 1.0 copy.42
  239.0 0.8 copy.35
  239.7 4.4 %all-to-all-start.2 = ((bf16[8,32,512]{2,1,0:T(8,128)(2,1)}), bf16[8,32,512]{2,1,0:T(8,128)(2,1)S(1)}, u32[]{:S(2)}, u32[]{:S(2)}) async-start(bf16[8,32,512]{2,1,0:T(8,128)(2,1)} %copy.35), calls=%async_computation.2 | async-start | bytes 524288 | tf_op jit(solution)/shard_map/all_to_all | solution.py:61
  244.2 7.5 %all-to-all-done.2 = bf16[8,32,512]{2,1,0:T(8,128)(2,1)S(1)} async-done(((bf16[8,32,512]{2,1,0:T(8,128)(2,1)}), bf16[8,32,512]{2,1,0:T(8,128)(2,1)S(1)}, u32[]{:S(2)}, u32[]{:S(2)}) %all-to-all-start.2) | async-done | bytes 262176 | tf_op jit(solution)/shard_map/all_to_all | solution.py:61
  251.7 0.1 reshape.99
  251.8 0.3 fusion.13
  252.1 0.6 copy.37
  252.8 21.5 %all_to_all.31 = f32[16,4,8,512]{3,2,1,0:T(8,128)S(1)} all-to-all(f32[16,4,8,512]{3,2,1,0:T(8,128)S(1)} %copy.37), channel_id=1, replica_groups=mesh['dp'=16,'expert'=8] {'dp'}, dimensions={0} | all-to-all | bytes 2097152 | tf_op jit(solution)/shard_map/all_to_all | solution.py:66
  274.3 1.0 fusion.12
  (26 shorter events, 0.5 us)
Async XLA Ops:
  6.5 56.9 %all-gather.3.cloned.1.call-start = ((), (), s32[]{:S(2)}) async-start(), calls=%async_computation.5 | async-start | bytes 4456448 | tf_op jit(solution)/shard_map/all_gather | solution.py:32
  8.1 67.3 %copy-start = (s32[8,4]{0,1:T(4,128)S(1)}, s32[8,4]{0,1:T(4,128)}, u32[]{:S(2)}) copy-start(s32[8,4]{0,1:T(4,128)} %param.16) | copy-start | bytes 388
  69.2 31.7 %copy-start.1 = (f32[1,512]{1,0:T(1,128)S(1)}, f32[1,512]{1,0:T(1,128)}, u32[]{:S(2)}) copy-start(f32[1,512]{1,0:T(1,128)} %param.15) | copy-start | bytes 6148
  69.3 32.4 %copy-start.5 = (s32[8]{0:T(128)S(1)}, s32[8]{0:T(128)}, u32[]{:S(2)}) copy-start(s32[8]{0:T(128)} %param.17) | copy-start | bytes 100
  70.1 16.8 %all-to-all-start = ((bf16[16,4,8,512]{3,2,1,0:T(8,128)(2,1)}), bf16[16,4,8,512]{3,2,1,0:T(8,128)(2,1)S(1)}, u32[]{:S(2)}, u32[]{:S(2)}) async-start(bf16[16,4,8,512]{3,2,1,0:T(8,128)(2,1)} %bitcast.60), calls=%async_computation | async-start | bytes 1048576 | tf_op jit(solution)/shard_map/all_to_all | solution.py:37
  75.4 72.4 %all-gather.5.cloned.1.call-start = ((), (), s32[]{:S(2)}) async-start(), calls=%async_computation.6 | async-start | bytes 4456448 | tf_op jit(solution)/shard_map/all_gather | solution.py:43
  100.3 137.6 %reduce-scatter.4.cloned.1.call-start = ((), (), s32[]{:S(2)}) async-start(), calls=%async_computation.7 | async-start | bytes 4456448
  147.8 5.9 %copy-start.2 = (bf16[1,4096,512]{2,1,0:T(8,128)(2,1)S(1)}, bf16[1,4096,512]{2,1,0:T(8,128)(2,1)}, u32[]{:S(2)}) copy-start(bf16[1,4096,512]{2,1,0:T(8,128)(2,1)} %param.13) | copy-start | bytes 12582916
  147.8 5.9 %copy-start.4 = (bf16[512,4096]{1,0:T(8,128)(2,1)S(1)}, bf16[512,4096]{1,0:T(8,128)(2,1)}, u32[]{:S(2)}) copy-start(bf16[512,4096]{1,0:T(8,128)(2,1)} %all-gather.5.cloned.1.call-done) | copy-start | bytes 12582916
  153.8 2.5 copy-start.3
  239.7 11.9 %all-to-all-start.2 = ((bf16[8,32,512]{2,1,0:T(8,128)(2,1)}), bf16[8,32,512]{2,1,0:T(8,128)(2,1)S(1)}, u32[]{:S(2)}, u32[]{:S(2)}) async-start(bf16[8,32,512]{2,1,0:T(8,128)(2,1)} %copy.35), calls=%async_computation.2 | async-start | bytes 524288 | tf_op jit(solution)/shard_map/all_to_all | solution.py:61
Sparse Core Ops, SparseCore 0:
  9.5 53.8 all-gather.2
  100.4 47.3 all-gather.4
  160.7 77.1 reduce-scatter.3
where the time goes:
time: 282 us
  waiting for transfers between devices  197 us (70%)
  blocking collectives  33.3 us (12%)
  matrix products  18.9 us (7%)
  between operations  13.3 us (5%)
  starting transfers between devices  9.73 us (3%)
  local copies, waits for them, and re-layouts  7.46 us (3%)
    unnamed x4, waiting for transfers between devices  78.1 us
    all_gather x1, waiting for transfers between devices, body(): lax.all_gather(out_weight, 'dp', axis=0, tiled=True)  55.3 us
    all_gather x1, waiting for transfers between devices, body(): picked = lax.all_gather(mine, 'dp', axis=0, tiled=True)  44.6 us
    all_to_all x1, blocking collectives, body(): back = lax.all_to_all(added, 'dp', 0, 0, tiled=True)  21.5 us
    all_to_all x1, blocking collectives, body(): mine = lax.all_to_all(slots, 'expert', 0, 3, tiled=True)  11.8 us
    all_to_all x1, waiting for transfers between devices, body(): pieces = lax.all_to_all(split, 'dp', 0, 0, tiled=True)  11.3 us
    all_to_all x1, waiting for transfers between devices, body(): outs = lax.all_to_all(summed, 'expert', 0, 0, tiled=True)  7.45 us
    dot_general x1, matrix products, body(): gate = jnp.dot(picked, w_gate, preferred_element_type=jnp.float32)  5.92 us
  transfers between devices with their start and end apart: 5, of which 5 were waited for; matrix products, arithmetic and copies ran while one was open for 1% of the time, Pallas kernels for 0%

commit v1 on v0

--- a/solution.py
+++ b/solution.py
@@ -5,6 +5,27 @@
 
 BLK = 128
 CAP = 4
+
+
+def ring_gather(x, axis, dim):
+    count, place, width = (lax.axis_size(axis), lax.axis_index(axis), x.shape[dim])
+    forward = [(i, (i + 1) % count) for i in range(count)]
+    downward = [(i, (i - 1) % count) for i in range(count)]
+    out = jnp.zeros((*x.shape[:dim], count * width, *x.shape[dim + 1 :]), x.dtype)
+    out = lax.dynamic_update_slice_in_dim(out, x, place * width, axis=dim)
+    from_left = from_right = x
+    halfway = count // 2
+    for step in range(1, halfway + 1):
+        from_left = lax.ppermute(from_left, axis, forward)
+        out = lax.dynamic_update_slice_in_dim(
+            out, from_left, (place - step) % count * width, axis=dim
+        )
+        if step < count - halfway:
+            from_right = lax.ppermute(from_right, axis, downward)
+            out = lax.dynamic_update_slice_in_dim(
+                out, from_right, (place + step) % count * width, axis=dim
+            )
+    return out
 
 
 def body(
@@ -28,9 +49,7 @@
     piece = BLK // n_dp
     my_expert = lax.axis_index("expert")
     projected = jnp.dot(
-        context,
-        lax.all_gather(out_weight, "dp", axis=0, tiled=True),
-        preferred_element_type=jnp.float32,
+        context, ring_gather(out_weight, "dp", 0), preferred_element_type=jnp.float32
     )
     attended = (residual.astype(jnp.float32) + projected).astype(jnp.bfloat16)
     split = attended.reshape(local_blocks, n_dp, piece, local_width).transpose(1, 0, 2, 3)

time: 282 us -> 305 us (1.082)
  starting transfers between devices: 9.73 us -> 47 us
  waiting for transfers between devices: 197 us -> 169 us
  local copies, waits for them, and re-layouts: 7.46 us -> 20.6 us
    all_gather x1 -> x0, waiting for transfers between devices: 55.3 us -> none  [body(): lax.all_gather(out_weight, 'dp', axis=0, tiled=True)]
    ppermute x0 -> x15, starting transfers between devices: none -> 38.8 us  [the longest x7 37.1 us: ring_gather(): from_right = lax.ppermute(from_right, axis, downward)]
    ppermute x0 -> x15, waiting for transfers between devices: none -> 29.8 us  [the longest x8 22.9 us: ring_gather(): from_left = lax.ppermute(from_left, axis, forward)]
    dynamic_update_slice x0 -> x16, local copies, waits for them, and re-layouts: none -> 11.6 us  [the longest x8 5.81 us: ring_gather(): lax.dynamic_update_slice_in_dim(out, from_left, (place - step) % count *...]
    unnamed x4 -> x3, waiting for transfers between devices: 78.1 us -> 77.5 us
  transfers between devices with their start and end apart: 5 -> 19, of which waited for: 5 -> 13; matrix products, arithmetic and copies ran while one was open for 1% -> 5% of each run, Pallas kernels for 0% -> 0%
where the time goes in v1:
time: 305 us; the launch traced here: 304 us
  waiting for transfers between devices  169 us (55%)
  starting transfers between devices  47 us (15%)
  blocking collectives  34 us (11%)
  local copies, waits for them, and re-layouts  20.6 us (7%)
  matrix products  17.6 us (6%)
  between operations  13.6 us (4%)
    unnamed x3, waiting for transfers between devices  77.5 us
    all_gather x1, waiting for transfers between devices, body(): picked = lax.all_gather(mine, 'dp', axis=0, tiled=True)  44.6 us
    ppermute x7, starting transfers between devices, ring_gather(): from_right = lax.ppermute(from_right, axis, downward)  37.1 us
    ppermute x8, waiting for transfers between devices, ring_gather(): from_left = lax.ppermute(from_left, axis, forward)  22.9 us
    all_to_all x1, blocking collectives, body(): back = lax.all_to_all(added, 'dp', 0, 0, tiled=True)  21.5 us
    all_to_all x1, blocking collectives, body(): mine = lax.all_to_all(slots, 'expert', 0, 3, tiled=True)  12.6 us
    all_to_all x1, waiting for transfers between devices, body(): pieces = lax.all_to_all(split, 'dp', 0, 0, tiled=True)  9.88 us
    all_to_all x1, waiting for transfers between devices, body(): outs = lax.all_to_all(summed, 'expert', 0, 0, tiled=True)  7.45 us
  transfers between devices with their start and end apart: 19, of which 13 were waited for; matrix products, arithmetic and copies ran while one was open for 5% of the time, Pallas kernels for 0%

profile of v1, /device:TPU:0, one launch (start us, length us, event | category | flops | bytes accessed | tf_op | source)
XLA Modules:
  0.0 304.4 jit_solution(12259398340522167051)
XLA Ops:
  6.5 1.7 collective-permute-start
  8.2 3.7 %collective-permute-start.1 = (bf16[256,512]{1,0:T(8,128)(2,1)}, bf16[256,512]{1,0:T(8,128)(2,1)S(1)}, u32[]{:S(2)}, u32[]{:S(2)}) collective-permute-start(bf16[256,512]{1,0:T(8,128)(2,1)} %param.10), channel_id=1, source_target_pairs={{0,120},{8,0},{16,8},{24,16},{32,24},{40,32},{48,40},{56,48},{64,5... | collective-permute-start | bytes 786440 | tf_op jit(solution)/shard_map/ppermute | solution.py:24
  11.9 6.5 %collective-permute-done = bf16[256,512]{1,0:T(8,128)(2,1)S(1)} collective-permute-done((bf16[256,512]{1,0:T(8,128)(2,1)}, bf16[256,512]{1,0:T(8,128)(2,1)S(1)}, u32[]{:S(2)}, u32[]{:S(2)}) %collective-permute-start) | collective-permute-done | bytes 262176 | tf_op jit(solution)/shard_map/ppermute | solution.py:19
  18.4 5.3 %collective-permute-start.3 = (bf16[256,512]{1,0:T(8,128)(2,1)S(1)}, bf16[256,512]{1,0:T(8,128)(2,1)S(1)}, u32[]{:S(2)}, u32[]{:S(2)}) collective-permute-start(bf16[256,512]{1,0:T(8,128)(2,1)S(1)} %collective-permute-done.1), channel_id=1, source_target_pairs={{0,120},{8,0},{16,8},{24,16},{32,24},{40,32},{48,40},{56,48},{64,5... | collective-permute-start | bytes 786440 | tf_op jit(solution)/shard_map/ppermute | solution.py:24
  23.8 5.5 %collective-permute-done.2 = bf16[256,512]{1,0:T(8,128)(2,1)S(1)} collective-permute-done((bf16[256,512]{1,0:T(8,128)(2,1)S(1)}, bf16[256,512]{1,0:T(8,128)(2,1)S(1)}, u32[]{:S(2)}, u32[]{:S(2)}) %collective-permute-start.2) | collective-permute-done | bytes 262176 | tf_op jit(solution)/shard_map/ppermute | solution.py:19
  29.2 5.3 %collective-permute-start.5 = (bf16[256,512]{1,0:T(8,128)(2,1)S(1)}, bf16[256,512]{1,0:T(8,128)(2,1)S(1)}, u32[]{:S(2)}, u32[]{:S(2)}) collective-permute-start(bf16[256,512]{1,0:T(8,128)(2,1)S(1)} %collective-permute-done.3), channel_id=1, source_target_pairs={{0,120},{8,0},{16,8},{24,16},{32,24},{40,32},{48,40},{56,48},{64,5... | collective-permute-start | bytes 786440 | tf_op jit(solution)/shard_map/ppermute | solution.py:24
  34.6 4.5 %collective-permute-done.4 = bf16[256,512]{1,0:T(8,128)(2,1)S(1)} collective-permute-done((bf16[256,512]{1,0:T(8,128)(2,1)S(1)}, bf16[256,512]{1,0:T(8,128)(2,1)S(1)}, u32[]{:S(2)}, u32[]{:S(2)}) %collective-permute-start.4) | collective-permute-done | bytes 262176 | tf_op jit(solution)/shard_map/ppermute | solution.py:19
  39.1 2.2 broadcast_in_dim.17
  43.0 5.3 %collective-permute-start.7 = (bf16[256,512]{1,0:T(8,128)(2,1)S(1)}, bf16[256,512]{1,0:T(8,128)(2,1)S(1)}, u32[]{:S(2)}, u32[]{:S(2)}) collective-permute-start(bf16[256,512]{1,0:T(8,128)(2,1)S(1)} %collective-permute-done.5), channel_id=1, source_target_pairs={{0,120},{8,0},{16,8},{24,16},{32,24},{40,32},{48,40},{56,48},{64,5... | collective-permute-start | bytes 786440 | tf_op jit(solution)/shard_map/ppermute | solution.py:24
  50.5 1.7 collective-permute-done.7
  52.2 5.8 %collective-permute-start.9 = (bf16[256,512]{1,0:T(8,128)(2,1)S(1)}, bf16[256,512]{1,0:T(8,128)(2,1)S(1)}, u32[]{:S(2)}, u32[]{:S(2)}) collective-permute-start(bf16[256,512]{1,0:T(8,128)(2,1)S(1)} %collective-permute-done.7), channel_id=1, source_target_pairs={{0,120},{8,0},{16,8},{24,16},{32,24},{40,32},{48,40},{56,48},{64,5... | collective-permute-start | bytes 786440 | tf_op jit(solution)/shard_map/ppermute | solution.py:24
  60.2 1.7 collective-permute-done.9
  61.9 5.8 %collective-permute-start.11 = (bf16[256,512]{1,0:T(8,128)(2,1)S(1)}, bf16[256,512]{1,0:T(8,128)(2,1)S(1)}, u32[]{:S(2)}, u32[]{:S(2)}) collective-permute-start(bf16[256,512]{1,0:T(8,128)(2,1)S(1)} %collective-permute-done.9), channel_id=1, source_target_pairs={{0,120},{8,0},{16,8},{24,16},{32,24},{40,32},{48,40},{56,48},{64,5... | collective-permute-start | bytes 786440 | tf_op jit(solution)/shard_map/ppermute | solution.py:24
  69.9 2.0 collective-permute-done.11
  71.9 5.8 %collective-permute-start.13 = (bf16[256,512]{1,0:T(8,128)(2,1)S(1)}, bf16[256,512]{1,0:T(8,128)(2,1)S(1)}, u32[]{:S(2)}, u32[]{:S(2)}) collective-permute-start(bf16[256,512]{1,0:T(8,128)(2,1)S(1)} %collective-permute-done.11), channel_id=1, source_target_pairs={{0,120},{8,0},{16,8},{24,16},{32,24},{40,32},{48,40},{56,48},{64,5... | collective-permute-start | bytes 786440 | tf_op jit(solution)/shard_map/ppermute | solution.py:24
  80.2 1.4 collective-permute-done.13
  82.3 6.1 %collective-permute-done.14 = bf16[256,512]{1,0:T(8,128)(2,1)S(1)} collective-permute-done((bf16[256,512]{1,0:T(8,128)(2,1)S(1)}, bf16[256,512]{1,0:T(8,128)(2,1)S(1)}, u32[]{:S(2)}, u32[]{:S(2)}) %collective-permute-start.14) | collective-permute-done | bytes 262176 | tf_op jit(solution)/shard_map/ppermute | solution.py:19
  89.1 4.5 %fusion.9 = bf16[512,512]{1,0:T(8,128)(2,1)S(1)} fusion(bf16[512,4096]{1,0:T(8,128)(2,1)S(1)} %copy-done.3, bf16[4096,512]{1,0:T(8,128)(2,1)} %constant_dynamic-update-slice_fusion, bf16[512,512]{1,0:T(8,128)(2,1)S(1)} %copy-done.7), kind=kOutput, calls=%fused_computation.10 | convolution fusion | flops 2148270080 | bytes 9437184 | tf_op jit(solution)/shard_map/dot_general | solution.py:51
  93.7 0.9 copy.49
  94.6 3.6 %all-to-all-start = ((bf16[16,4,8,512]{3,2,1,0:T(8,128)(2,1)}), bf16[16,4,8,512]{3,2,1,0:T(8,128)(2,1)S(1)}, u32[]{:S(2)}, u32[]{:S(2)}) async-start(bf16[16,4,8,512]{3,2,1,0:T(8,128)(2,1)} %bitcast.66), calls=%async_computation | async-start | bytes 1048576 | tf_op jit(solution)/shard_map/all_to_all | solution.py:56
  98.3 9.9 %all-to-all-done = bf16[16,4,8,512]{3,2,1,0:T(8,128)(2,1)S(1)} async-done(((bf16[16,4,8,512]{3,2,1,0:T(8,128)(2,1)}), bf16[16,4,8,512]{3,2,1,0:T(8,128)(2,1)S(1)}, u32[]{:S(2)}, u32[]{:S(2)}) %all-to-all-start) | async-done | bytes 524320 | tf_op jit(solution)/shard_map/all_to_all | solution.py:56
  108.9 12.6 %all_to_all.30 = bf16[8,4,8,512]{3,2,1,0:T(8,128)(2,1)S(1)} all-to-all(bf16[8,4,8,512]{3,2,1,0:T(8,128)(2,1)S(1)} %broadcast_select_fusion), channel_id=1, replica_groups=mesh['dp'=16,'expert'=8] {'expert'}, dimensions={0} | all-to-all | bytes 524288 | tf_op jit(solution)/shard_map/all_to_all | solution.py:60
  125.3 44.6 %all-gather.2.cloned.1.call-done = bf16[512,4096]{1,0:T(8,128)(2,1)} async-done(((bf16[32,4096]{1,0:T(8,128)(2,1)}), bf16[512,4096]{1,0:T(8,128)(2,1)}) %all-gather.2.cloned.1.call-update) | async-done | bytes 4194320 | tf_op jit(solution)/shard_map/all_gather | solution.py:62
  169.9 5.9 %fusion.3 = f32[512,512]{1,0:T(8,128)S(1)} fusion(bf16[512,4096]{1,0:T(8,128)(2,1)} %all-gather.2.cloned.1.call-done, bf16[1,4096,512]{2,1,0:T(8,128)(2,1)} %param.12), kind=kOutput, calls=%fused_computation.5 | convolution fusion | flops 2147483648 | bytes 9437184 | tf_op jit(solution)/shard_map/dot_general | solution.py:71
  175.9 2.4 fusion.10
  178.3 4.3 %multiply_convert_fusion = bf16[512,4096]{1,0:T(8,128)(2,1)} fusion(bf16[512,512]{1,0:T(8,128)(2,1)S(1)} %fusion.10, bf16[1,512,4096]{2,1,0:T(8,128)(2,1)S(1)} %copy-done.5, f32[512]{0:T(512)S(1)} %mul.83), kind=kOutput, calls=%fused_computation.1 | convolution fusion | flops 2151677952 | bytes 8914944 | tf_op jit(solution)/shard_map/dot_general | solution.py:74
  182.7 77.4 %reduce-scatter.4.cloned.1.call-done = bf16[1,32,4096]{2,1,0:T(8,128)(2,1)} async-done(((bf16[16,32,4096]{2,1,0:T(8,128)(2,1)}), bf16[1,32,4096]{2,1,0:T(8,128)(2,1)}) %reduce-scatter.4.cloned.1.call-update) | async-done | bytes 262160
  260.1 1.0 copy.42
  261.9 4.4 %all-to-all-start.2 = ((bf16[8,32,512]{2,1,0:T(8,128)(2,1)}), bf16[8,32,512]{2,1,0:T(8,128)(2,1)S(1)}, u32[]{:S(2)}, u32[]{:S(2)}) async-start(bf16[8,32,512]{2,1,0:T(8,128)(2,1)} %copy.35), calls=%async_computation.2 | async-start | bytes 524288 | tf_op jit(solution)/shard_map/all_to_all | solution.py:80
  266.5 7.5 %all-to-all-done.2 = bf16[8,32,512]{2,1,0:T(8,128)(2,1)S(1)} async-done(((bf16[8,32,512]{2,1,0:T(8,128)(2,1)}), bf16[8,32,512]{2,1,0:T(8,128)(2,1)S(1)}, u32[]{:S(2)}, u32[]{:S(2)}) %all-to-all-start.2) | async-done | bytes 262176 | tf_op jit(solution)/shard_map/all_to_all | solution.py:80
  275.0 21.5 %all_to_all.31 = f32[16,4,8,512]{3,2,1,0:T(8,128)S(1)} all-to-all(f32[16,4,8,512]{3,2,1,0:T(8,128)S(1)} %copy.37), channel_id=1, replica_groups=mesh['dp'=16,'expert'=8] {'dp'}, dimensions={0} | all-to-all | bytes 2097152 | tf_op jit(solution)/shard_map/all_to_all | solution.py:85
  296.6 1.0 fusion.13
  (76 shorter events, 18.8 us)
Async XLA Ops:
  6.5 34.8 %copy-start = (bf16[256,512]{1,0:T(8,128)(2,1)S(1)}, bf16[256,512]{1,0:T(8,128)(2,1)}, u32[]{:S(2)}) copy-start(bf16[256,512]{1,0:T(8,128)(2,1)} %param.10) | copy-start | bytes 786436
  6.5 35.5 %copy-start.1 = (s32[8,4]{0,1:T(4,128)S(1)}, s32[8,4]{0,1:T(4,128)}, u32[]{:S(2)}) copy-start(s32[8,4]{0,1:T(4,128)} %param.16) | copy-start | bytes 388
  6.5 11.9 %collective-permute-start = (bf16[256,512]{1,0:T(8,128)(2,1)}, bf16[256,512]{1,0:T(8,128)(2,1)S(1)}, u32[]{:S(2)}, u32[]{:S(2)}) collective-permute-start(bf16[256,512]{1,0:T(8,128)(2,1)} %param.10), channel_id=1, source_target_pairs={{0,8},{8,16},{16,24},{24,32},{32,40},{40,48},{48,56},{56,64},{64,7... | collective-permute-start | bytes 786440 | tf_op jit(solution)/shard_map/ppermute | solution.py:19
  8.2 10.2 %collective-permute-start.1 = (bf16[256,512]{1,0:T(8,128)(2,1)}, bf16[256,512]{1,0:T(8,128)(2,1)S(1)}, u32[]{:S(2)}, u32[]{:S(2)}) collective-permute-start(bf16[256,512]{1,0:T(8,128)(2,1)} %param.10), channel_id=1, source_target_pairs={{0,120},{8,0},{16,8},{24,16},{32,24},{40,32},{48,40},{56,48},{64,5... | collective-permute-start | bytes 786440 | tf_op jit(solution)/shard_map/ppermute | solution.py:24
  18.4 10.8 %collective-permute-start.2 = (bf16[256,512]{1,0:T(8,128)(2,1)S(1)}, bf16[256,512]{1,0:T(8,128)(2,1)S(1)}, u32[]{:S(2)}, u32[]{:S(2)}) collective-permute-start(bf16[256,512]{1,0:T(8,128)(2,1)S(1)} %collective-permute-done), channel_id=1, source_target_pairs={{0,8},{8,16},{16,24},{24,32},{32,40},{40,48},{48,56},{56,64},{64,7... | collective-permute-start | bytes 786440 | tf_op jit(solution)/shard_map/ppermute | solution.py:19
  18.4 10.8 %collective-permute-start.3 = (bf16[256,512]{1,0:T(8,128)(2,1)S(1)}, bf16[256,512]{1,0:T(8,128)(2,1)S(1)}, u32[]{:S(2)}, u32[]{:S(2)}) collective-permute-start(bf16[256,512]{1,0:T(8,128)(2,1)S(1)} %collective-permute-done.1), channel_id=1, source_target_pairs={{0,120},{8,0},{16,8},{24,16},{32,24},{40,32},{48,40},{56,48},{64,5... | collective-permute-start | bytes 786440 | tf_op jit(solution)/shard_map/ppermute | solution.py:24
  29.2 9.9 %collective-permute-start.4 = (bf16[256,512]{1,0:T(8,128)(2,1)S(1)}, bf16[256,512]{1,0:T(8,128)(2,1)S(1)}, u32[]{:S(2)}, u32[]{:S(2)}) collective-permute-start(bf16[256,512]{1,0:T(8,128)(2,1)S(1)} %collective-permute-done.2), channel_id=1, source_target_pairs={{0,8},{8,16},{16,24},{24,32},{32,40},{40,48},{48,56},{56,64},{64,7... | collective-permute-start | bytes 786440 | tf_op jit(solution)/shard_map/ppermute | solution.py:19
  29.2 13.8 %collective-permute-start.5 = (bf16[256,512]{1,0:T(8,128)(2,1)S(1)}, bf16[256,512]{1,0:T(8,128)(2,1)S(1)}, u32[]{:S(2)}, u32[]{:S(2)}) collective-permute-start(bf16[256,512]{1,0:T(8,128)(2,1)S(1)} %collective-permute-done.3), channel_id=1, source_target_pairs={{0,120},{8,0},{16,8},{24,16},{32,24},{40,32},{48,40},{56,48},{64,5... | collective-permute-start | bytes 786440 | tf_op jit(solution)/shard_map/ppermute | solution.py:24
  39.1 9.9 %collective-permute-start.6 = (bf16[256,512]{1,0:T(8,128)(2,1)S(1)}, bf16[256,512]{1,0:T(8,128)(2,1)S(1)}, u32[]{:S(2)}, u32[]{:S(2)}) collective-permute-start(bf16[256,512]{1,0:T(8,128)(2,1)S(1)} %collective-permute-done.4), channel_id=1, source_target_pairs={{0,8},{8,16},{16,24},{24,32},{32,40},{40,48},{48,56},{56,64},{64,7... | collective-permute-start | bytes 786440 | tf_op jit(solution)/shard_map/ppermute | solution.py:19
  42.1 47.1 %copy-start.7 = (bf16[512,512]{1,0:T(8,128)(2,1)S(1)}, bf16[512,512]{1,0:T(8,128)(2,1)}, u32[]{:S(2)}) copy-start(bf16[512,512]{1,0:T(8,128)(2,1)} %param.11) | copy-start | bytes 1572868
  42.3 46.9 %copy-start.3 = (bf16[512,4096]{1,0:T(8,128)(2,1)S(1)}, bf16[512,4096]{1,0:T(8,128)(2,1)}, u32[]{:S(2)}) copy-start(bf16[512,4096]{1,0:T(8,128)(2,1)} %param.9) | copy-start | bytes 12582916
  43.0 9.2 %collective-permute-start.7 = (bf16[256,512]{1,0:T(8,128)(2,1)S(1)}, bf16[256,512]{1,0:T(8,128)(2,1)S(1)}, u32[]{:S(2)}, u32[]{:S(2)}) collective-permute-start(bf16[256,512]{1,0:T(8,128)(2,1)S(1)} %collective-permute-done.5), channel_id=1, source_target_pairs={{0,120},{8,0},{16,8},{24,16},{32,24},{40,32},{48,40},{56,48},{64,5... | collective-permute-start | bytes 786440 | tf_op jit(solution)/shard_map/ppermute | solution.py:24
  49.0 9.7 %collective-permute-start.8 = (bf16[256,512]{1,0:T(8,128)(2,1)S(1)}, bf16[256,512]{1,0:T(8,128)(2,1)S(1)}, u32[]{:S(2)}, u32[]{:S(2)}) collective-permute-start(bf16[256,512]{1,0:T(8,128)(2,1)S(1)} %collective-permute-done.6), channel_id=1, source_target_pairs={{0,8},{8,16},{16,24},{24,32},{32,40},{40,48},{48,56},{56,64},{64,7... | collective-permute-start | bytes 786440 | tf_op jit(solution)/shard_map/ppermute | solution.py:19
  52.2 9.7 %collective-permute-start.9 = (bf16[256,512]{1,0:T(8,128)(2,1)S(1)}, bf16[256,512]{1,0:T(8,128)(2,1)S(1)}, u32[]{:S(2)}, u32[]{:S(2)}) collective-permute-start(bf16[256,512]{1,0:T(8,128)(2,1)S(1)} %collective-permute-done.7), channel_id=1, source_target_pairs={{0,120},{8,0},{16,8},{24,16},{32,24},{40,32},{48,40},{56,48},{64,5... | collective-permute-start | bytes 786440 | tf_op jit(solution)/shard_map/ppermute | solution.py:24
  58.8 9.7 %collective-permute-start.10 = (bf16[256,512]{1,0:T(8,128)(2,1)S(1)}, bf16[256,512]{1,0:T(8,128)(2,1)S(1)}, u32[]{:S(2)}, u32[]{:S(2)}) collective-permute-start(bf16[256,512]{1,0:T(8,128)(2,1)S(1)} %collective-permute-done.8), channel_id=1, source_target_pairs={{0,8},{8,16},{16,24},{24,32},{32,40},{40,48},{48,56},{56,64},{64,7... | collective-permute-start | bytes 786440 | tf_op jit(solution)/shard_map/ppermute | solution.py:19
  61.9 10.0 %collective-permute-start.11 = (bf16[256,512]{1,0:T(8,128)(2,1)S(1)}, bf16[256,512]{1,0:T(8,128)(2,1)S(1)}, u32[]{:S(2)}, u32[]{:S(2)}) collective-permute-start(bf16[256,512]{1,0:T(8,128)(2,1)S(1)} %collective-permute-done.9), channel_id=1, source_target_pairs={{0,120},{8,0},{16,8},{24,16},{32,24},{40,32},{48,40},{56,48},{64,5... | collective-permute-start | bytes 786440 | tf_op jit(solution)/shard_map/ppermute | solution.py:24
  68.4 10.3 %collective-permute-start.12 = (bf16[256,512]{1,0:T(8,128)(2,1)S(1)}, bf16[256,512]{1,0:T(8,128)(2,1)S(1)}, u32[]{:S(2)}, u32[]{:S(2)}) collective-permute-start(bf16[256,512]{1,0:T(8,128)(2,1)S(1)} %collective-permute-done.10), channel_id=1, source_target_pairs={{0,8},{8,16},{16,24},{24,32},{32,40},{40,48},{48,56},{56,64},{64,7... | collective-permute-start | bytes 786440 | tf_op jit(solution)/shard_map/ppermute | solution.py:19
  71.9 9.7 %collective-permute-start.13 = (bf16[256,512]{1,0:T(8,128)(2,1)S(1)}, bf16[256,512]{1,0:T(8,128)(2,1)S(1)}, u32[]{:S(2)}, u32[]{:S(2)}) collective-permute-start(bf16[256,512]{1,0:T(8,128)(2,1)S(1)} %collective-permute-done.11), channel_id=1, source_target_pairs={{0,120},{8,0},{16,8},{24,16},{32,24},{40,32},{48,40},{56,48},{64,5... | collective-permute-start | bytes 786440 | tf_op jit(solution)/shard_map/ppermute | solution.py:24
  78.7 9.7 %collective-permute-start.14 = (bf16[256,512]{1,0:T(8,128)(2,1)S(1)}, bf16[256,512]{1,0:T(8,128)(2,1)S(1)}, u32[]{:S(2)}, u32[]{:S(2)}) collective-permute-start(bf16[256,512]{1,0:T(8,128)(2,1)S(1)} %collective-permute-done.12), channel_id=1, source_target_pairs={{0,8},{8,16},{16,24},{24,32},{32,40},{40,48},{48,56},{56,64},{64,7... | collective-permute-start | bytes 786440 | tf_op jit(solution)/shard_map/ppermute | solution.py:19
  93.7 29.5 %copy-start.2 = (f32[1,512]{1,0:T(1,128)S(1)}, f32[1,512]{1,0:T(1,128)}, u32[]{:S(2)}) copy-start(f32[1,512]{1,0:T(1,128)} %param.15) | copy-start | bytes 6148
  93.7 30.2 %copy-start.8 = (s32[8]{0:T(128)S(1)}, s32[8]{0:T(128)}, u32[]{:S(2)}) copy-start(s32[8]{0:T(128)} %param.17) | copy-start | bytes 100
  94.6 13.6 %all-to-all-start = ((bf16[16,4,8,512]{3,2,1,0:T(8,128)(2,1)}), bf16[16,4,8,512]{3,2,1,0:T(8,128)(2,1)S(1)}, u32[]{:S(2)}, u32[]{:S(2)}) async-start(bf16[16,4,8,512]{3,2,1,0:T(8,128)(2,1)} %bitcast.66), calls=%async_computation | async-start | bytes 1048576 | tf_op jit(solution)/shard_map/all_to_all | solution.py:56
  98.1 71.8 %all-gather.2.cloned.1.call-start = ((), (), s32[]{:S(2)}) async-start(), calls=%async_computation.5 | async-start | bytes 4456448 | tf_op jit(solution)/shard_map/all_gather | solution.py:62
  122.4 137.7 %reduce-scatter.4.cloned.1.call-start = ((), (), s32[]{:S(2)}) async-start(), calls=%async_computation.6 | async-start | bytes 4456448
  169.9 5.9 %copy-start.4 = (bf16[1,4096,512]{2,1,0:T(8,128)(2,1)S(1)}, bf16[1,4096,512]{2,1,0:T(8,128)(2,1)}, u32[]{:S(2)}) copy-start(bf16[1,4096,512]{2,1,0:T(8,128)(2,1)} %param.13) | copy-start | bytes 12582916
  169.9 5.9 %copy-start.6 = (bf16[512,4096]{1,0:T(8,128)(2,1)S(1)}, bf16[512,4096]{1,0:T(8,128)(2,1)}, u32[]{:S(2)}) copy-start(bf16[512,4096]{1,0:T(8,128)(2,1)} %all-gather.2.cloned.1.call-done) | copy-start | bytes 12582916
  175.9 2.5 copy-start.5
  261.9 12.0 %all-to-all-start.2 = ((bf16[8,32,512]{2,1,0:T(8,128)(2,1)}), bf16[8,32,512]{2,1,0:T(8,128)(2,1)S(1)}, u32[]{:S(2)}, u32[]{:S(2)}) async-start(bf16[8,32,512]{2,1,0:T(8,128)(2,1)} %copy.35), calls=%async_computation.2 | async-start | bytes 524288 | tf_op jit(solution)/shard_map/all_to_all | solution.py:80
Sparse Core Ops, SparseCore 0:
  122.5 47.3 all-gather.1
  182.8 77.2 reduce-scatter.3
